TPU v7x, 256 devices: a whole 4x4x8 slice. The times are simulated.
256 devices in a mesh: ctx: 16 (over z, x_lo), seq: 16 (over y, x_hi, core).
Axes of the slice: x: 4 (x_hi: 2, x_lo: 2; x = x_hi * 2 + x_lo), y: 4, z: 8, core: 2. Of those that a mesh axis runs over, the one named last changes fastest.
Arguments:
- normed_hidden_input: bfloat16 [16, 2048, 4096], P('seq', 'ctx'), may hold values from -6 to 6
- frozen_query_base: bfloat16 [16, 2048, 2048], P('seq', 'ctx'), may hold values from -6 to 6
- key_head_states: bfloat16 [16, 2048, 512], P('seq', 'ctx'), may hold values from -6 to 6
- value_head_states: bfloat16 [16, 2048, 512], P('seq', 'ctx'), may hold values from -6 to 6
- document_numbers: int32 [16, 2048], P('seq', 'ctx'), may hold values from 0 to 3, as said below
- tenant_block_entry: int32 [16, 64], P('seq', 'ctx'), may hold values from 0 to 5
- sequence_adapter_list: int32 [16, 6], replicated, may hold values from 0 to 15, as said below
- adapter_down_weight: bfloat16 [16, 64, 4096], P('seq', None, 'ctx'), may hold values from -0.09375 to 0.09375
- adapter_up_weight: bfloat16 [16, 64, 2048], P('seq', None, 'ctx'), may hold values from -0.75 to 0.75
- output_gradient: bfloat16 [16, 2048, 2048], P('seq', 'ctx'), may hold values from -6 to 6
Outputs:
- attention_out: bfloat16 [16, 2048, 2048], P('seq', 'ctx')
- key_grad: float32 [16, 2048, 512], P('seq', 'ctx')
- value_grad: float32 [16, 2048, 512], P('seq', 'ctx')
- down_grad: float32 [16, 64, 4096], P('seq', None, 'ctx')
- up_grad: float32 [16, 64, 2048], P('seq', None, 'ctx')
Inputs may be any that keep to these rules, and one draw needn't show every extreme that they name: `document_numbers`: each sequence is cut into 4 documents of consecutive positions, numbered in order; every document starts at an even position and has 2 or more positions. `sequence_adapter_list`: each row lists 6 different tenants.
All inputs are finite; a program needn't handle non-finite values.
Results may differ from a plain program's by a relative error of at most 0.04.
Values may be sent and summed in bfloat16 or wider, within the bound.
A program may use at most 128 MiB of HBM per device.

v0:
```python
import math
import jax
import jax.numpy as jnp
from jax import lax
from jax.sharding import PartitionSpec as P

MODEL_WIDTH = 4096
QUERY_HEADS = 16
KEY_VALUE_HEADS = 4
HEAD_SIZE = 128
ADAPTER_RANK = 64
TB = 32
PICK = 6
masked_fill_value = -1e30


def forward_block(
    running,
    query_head_rows,
    query_pos,
    query_doc,
    key_block,
    value_block,
    doc_block,
    key_pos,
    score_scale,
):
    row_peak, weight_total, mixed_sum = running
    scores = (
        jnp.einsum("tkgd,skd->kgts", query_head_rows, key_block, preferred_element_type=jnp.float32)
        * score_scale
    )
    allowed = (query_doc[:, None] == doc_block[None, :]) & (key_pos[None, :] <= query_pos[:, None])
    scores = jnp.where(allowed, scores, masked_fill_value)
    new_peak = jnp.maximum(row_peak, jnp.max(scores, axis=-1))
    weights = jnp.where(allowed, jnp.exp(scores - new_peak[..., None]), 0.0)
    factor = jnp.exp(row_peak - new_peak)
    weight_total = weight_total * factor + jnp.sum(weights, axis=-1)
    mixed_sum = mixed_sum * factor[..., None] + jnp.einsum(
        "kgts,skd->kgtd",
        weights.astype(jnp.bfloat16),
        value_block,
        preferred_element_type=jnp.float32,
    )
    return (new_peak, weight_total, mixed_sum)


def backward_block(
    query_head_rows,
    gradient_head_rows,
    query_pos,
    query_doc,
    log_total,
    delta_sum,
    key_block,
    value_block,
    doc_block,
    key_pos,
    score_scale,
):
    scores = (
        jnp.einsum("tkgd,skd->kgts", query_head_rows, key_block, preferred_element_type=jnp.float32)
        * score_scale
    )
    allowed = (query_doc[:, None] == doc_block[None, :]) & (key_pos[None, :] <= query_pos[:, None])
    probabilities = jnp.where(
        allowed, jnp.exp(jnp.where(allowed, scores, masked_fill_value) - log_total[..., None]), 0.0
    )
    value_part = jnp.einsum(
        "kgts,tkgd->skd",
        probabilities.astype(jnp.bfloat16),
        gradient_head_rows,
        preferred_element_type=jnp.float32,
    )
    dprobs = jnp.einsum(
        "tkgd,skd->kgts", gradient_head_rows, value_block, preferred_element_type=jnp.float32
    )
    dscores = (probabilities * (dprobs - delta_sum[..., None])).astype(jnp.bfloat16)
    query_part = score_scale * jnp.einsum(
        "kgts,skd->kgtd", dscores, key_block, preferred_element_type=jnp.float32
    )
    key_part = score_scale * jnp.einsum(
        "kgts,tkgd->skd", dscores, query_head_rows, preferred_element_type=jnp.float32
    )
    return (query_part, key_part, value_part)


def per_device(
    normed_hidden_input,
    frozen_query_base,
    key_head_states,
    value_head_states,
    document_numbers,
    tenant_block_entry,
    sequence_adapter_list,
    adapter_down_weight,
    adapter_up_weight,
    output_gradient,
):
    cycle_count = lax.axis_size("ctx")
    cycle_index = lax.axis_index("ctx")
    group_index = lax.axis_index("seq")
    tokens = normed_hidden_input[0]
    row_total_count = tokens.shape[0]
    seq_len = row_total_count * cycle_count
    head_groupings = QUERY_HEADS // KEY_VALUE_HEADS
    query_width = QUERY_HEADS * HEAD_SIZE
    key_feature_width = KEY_VALUE_HEADS * HEAD_SIZE
    score_scale = 1.0 / math.sqrt(HEAD_SIZE)
    down_portion = adapter_down_weight.shape[2]
    up_portion = adapter_up_weight.shape[2]
    owned_token_slices = jnp.concatenate([adapter_down_weight, adapter_up_weight], axis=2)
    every_slice = lax.all_gather(owned_token_slices, "seq", axis=0, tiled=True)
    selected_tenant = lax.dynamic_index_in_dim(
        sequence_adapter_list, group_index, 0, keepdims=False
    )
    picked = jnp.take(every_slice, selected_tenant, axis=0)
    spread = lax.all_gather(picked[None], "ctx", axis=0, tiled=True)
    down_full = jnp.transpose(spread[:, :, :, :down_portion], (1, 2, 0, 3)).reshape(
        PICK, ADAPTER_RANK, MODEL_WIDTH
    )
    up_full = jnp.transpose(spread[:, :, :, down_portion:], (1, 2, 0, 3)).reshape(
        PICK, ADAPTER_RANK, query_width
    )
    block_count = row_total_count // TB
    slot_ids = tenant_block_entry[0]
    down_blocks = jnp.take(down_full, slot_ids, axis=0)
    up_blocks = jnp.take(up_full, slot_ids, axis=0)
    token_blocks = tokens.reshape(block_count, TB, MODEL_WIDTH)
    low_rank = jnp.einsum(
        "btd,brd->btr", token_blocks, down_blocks, preferred_element_type=jnp.float32
    ).astype(jnp.bfloat16)
    lifted = jnp.einsum("btr,brq->btq", low_rank, up_blocks, preferred_element_type=jnp.float32)
    query_rows = (
        frozen_query_base[0].astype(jnp.float32) + lifted.reshape(row_total_count, query_width)
    ).astype(jnp.bfloat16)
    query_head_rows = query_rows.reshape(
        row_total_count, KEY_VALUE_HEADS, head_groupings, HEAD_SIZE
    )
    query_pos = cycle_index * row_total_count + jnp.arange(row_total_count, dtype=jnp.int32)
    query_doc = document_numbers[0]
    start_forward = (
        jnp.full(
            (KEY_VALUE_HEADS, head_groupings, row_total_count), masked_fill_value, jnp.float32
        ),
        jnp.zeros((KEY_VALUE_HEADS, head_groupings, row_total_count), jnp.float32),
        jnp.zeros((KEY_VALUE_HEADS, head_groupings, row_total_count, HEAD_SIZE), jnp.float32),
    )
    gathered = (
        lax.all_gather(key_head_states[0], "ctx", axis=0, tiled=True),
        lax.all_gather(value_head_states[0], "ctx", axis=0, tiled=True),
        lax.all_gather(document_numbers[0], "ctx", axis=0, tiled=True),
    )
    key_piece, value_piece, doc_piece = gathered
    length = key_piece.shape[0]
    tenant_block_width = math.gcd(length, 512)

    def forward_one_block(block_index, state_now):
        first_row = block_index * tenant_block_width
        key_block = lax.dynamic_slice_in_dim(key_piece, first_row, tenant_block_width, 0).reshape(
            tenant_block_width, KEY_VALUE_HEADS, HEAD_SIZE
        )
        value_block = lax.dynamic_slice_in_dim(
            value_piece, first_row, tenant_block_width, 0
        ).reshape(tenant_block_width, KEY_VALUE_HEADS, HEAD_SIZE)
        doc_block = lax.dynamic_slice_in_dim(doc_piece, first_row, tenant_block_width, 0)
        key_pos = 0 + first_row + jnp.arange(tenant_block_width, dtype=jnp.int32)
        return forward_block(
            state_now,
            query_head_rows,
            query_pos,
            query_doc,
            key_block,
            value_block,
            doc_block,
            key_pos,
            score_scale,
        )

    running = lax.fori_loop(0, length // tenant_block_width, forward_one_block, start_forward)
    row_peak, weight_total, mixed_sum = running
    attention_row_block = (
        (mixed_sum / weight_total[..., None])
        .transpose(2, 0, 1, 3)
        .reshape(row_total_count, query_width)
        .astype(jnp.bfloat16)
    )
    log_total = row_peak + jnp.log(weight_total)
    gradient_row_block = output_gradient[0]
    gradient_head_rows = gradient_row_block.reshape(
        row_total_count, KEY_VALUE_HEADS, head_groupings, HEAD_SIZE
    )
    output_head_rows = attention_row_block.reshape(
        row_total_count, KEY_VALUE_HEADS, head_groupings, HEAD_SIZE
    )
    delta_sum = jnp.einsum(
        "tkgd,tkgd->kgt", gradient_head_rows, output_head_rows, preferred_element_type=jnp.float32
    )
    start_backward = (
        jnp.zeros((KEY_VALUE_HEADS, head_groupings, row_total_count, HEAD_SIZE), jnp.float32),
        jnp.zeros((seq_len, key_feature_width), jnp.float32),
        jnp.zeros((seq_len, key_feature_width), jnp.float32),
    )
    backward_key_piece, backward_value_piece, backward_doc_piece = gathered
    length = backward_key_piece.shape[0]
    backward_tenant_block_width = math.gcd(length, 512)

    def backward_one_block(block_index, state_now):
        query_sum, key_gradient_sum, value_gradient_sum = state_now
        first_row = block_index * backward_tenant_block_width
        key_block = lax.dynamic_slice_in_dim(
            backward_key_piece, first_row, backward_tenant_block_width, 0
        ).reshape(backward_tenant_block_width, KEY_VALUE_HEADS, HEAD_SIZE)
        value_block = lax.dynamic_slice_in_dim(
            backward_value_piece, first_row, backward_tenant_block_width, 0
        ).reshape(backward_tenant_block_width, KEY_VALUE_HEADS, HEAD_SIZE)
        doc_block = lax.dynamic_slice_in_dim(
            backward_doc_piece, first_row, backward_tenant_block_width, 0
        )
        row_start = 0 + first_row
        key_pos = row_start + jnp.arange(backward_tenant_block_width, dtype=jnp.int32)
        query_part, key_part, value_part = backward_block(
            query_head_rows,
            gradient_head_rows,
            query_pos,
            query_doc,
            log_total,
            delta_sum,
            key_block,
            value_block,
            doc_block,
            key_pos,
            score_scale,
        )
        old_key = lax.dynamic_slice_in_dim(
            key_gradient_sum, row_start, backward_tenant_block_width, 0
        )
        key_gradient_sum = lax.dynamic_update_slice_in_dim(
            key_gradient_sum,
            old_key + key_part.reshape(backward_tenant_block_width, key_feature_width),
            row_start,
            0,
        )
        old_value = lax.dynamic_slice_in_dim(
            value_gradient_sum, row_start, backward_tenant_block_width, 0
        )
        value_gradient_sum = lax.dynamic_update_slice_in_dim(
            value_gradient_sum,
            old_value + value_part.reshape(backward_tenant_block_width, key_feature_width),
            row_start,
            0,
        )
        return (query_sum + query_part, key_gradient_sum, value_gradient_sum)

    backward_sums = lax.fori_loop(
        0, length // backward_tenant_block_width, backward_one_block, start_backward
    )
    query_sum, key_rows_grad, value_rows_grad = backward_sums
    query_grad_low = (
        query_sum.transpose(2, 0, 1, 3).reshape(row_total_count, query_width).astype(jnp.bfloat16)
    )
    grad_blocks = query_grad_low.reshape(block_count, TB, query_width)
    low_grad = jnp.einsum(
        "btq,brq->btr", grad_blocks, up_blocks, preferred_element_type=jnp.float32
    ).astype(jnp.bfloat16)
    up_grad_blocks = jnp.einsum(
        "btr,btq->brq", low_rank, grad_blocks, preferred_element_type=jnp.float32
    )
    down_grad_blocks = jnp.einsum(
        "btr,btd->brd", low_grad, token_blocks, preferred_element_type=jnp.float32
    )
    down_sum = (
        jnp.zeros((PICK, ADAPTER_RANK, MODEL_WIDTH), jnp.float32).at[slot_ids].add(down_grad_blocks)
    )
    up_sum = (
        jnp.zeros((PICK, ADAPTER_RANK, query_width), jnp.float32).at[slot_ids].add(up_grad_blocks)
    )
    adapter_terms = jnp.concatenate(
        [
            down_sum.reshape(PICK, ADAPTER_RANK, cycle_count, down_portion).transpose(2, 0, 1, 3),
            up_sum.reshape(PICK, ADAPTER_RANK, cycle_count, up_portion).transpose(2, 0, 1, 3),
        ],
        axis=3,
    )
    key_share, value_share, adapter_part = (
        lax.psum_scatter(key_rows_grad, "ctx", scatter_dimension=0, tiled=True),
        lax.psum_scatter(value_rows_grad, "ctx", scatter_dimension=0, tiled=True),
        lax.psum_scatter(adapter_terms, "ctx", scatter_dimension=0, tiled=True),
    )
    adapter_share = adapter_part[0]
    owner_table = (
        jnp.zeros((every_slice.shape[0], ADAPTER_RANK, adapter_share.shape[2]), jnp.float32)
        .at[selected_tenant]
        .set(adapter_share)
    )
    owner_share = lax.psum_scatter(owner_table, "seq", scatter_dimension=0, tiled=True)
    down_grad = owner_share[:, :, :down_portion]
    up_grad = owner_share[:, :, down_portion:]
    return (attention_row_block[None], key_share[None], value_share[None], down_grad, up_grad)


def solution(mesh):
    in_specs = (
        P("seq", "ctx", None),
        P("seq", "ctx", None),
        P("seq", "ctx", None),
        P("seq", "ctx", None),
        P("seq", "ctx"),
        P("seq", "ctx"),
        P(),
        P("seq", None, "ctx"),
        P("seq", None, "ctx"),
        P("seq", "ctx", None),
    )
    out_specs = (
        P("seq", "ctx", None),
        P("seq", "ctx", None),
        P("seq", "ctx", None),
        P("seq", None, "ctx"),
        P("seq", None, "ctx"),
    )
    return jax.shard_map(
        per_device, mesh=mesh, in_specs=in_specs, out_specs=out_specs, check_vma=False
    )
```

profile of v0, /device:TPU:8, one launch (start us, length us, event | category | flops | bytes accessed | tf_op | source)
XLA Modules:
  0.0 1046.2 jit_solution(15468660724500184358)
XLA Ops:
  9.0 24.9 %all_gather.17 = bf16[16,64,384]{2,1,0:T(8,128)(2,1)S(1)} all-gather(bf16[1,64,384]{2,1,0:T(8,128)(2,1)S(1)} %pad_maximum_fusion.1), channel_id=1, replica_groups=mesh['ctx'=16,'seq'=16] {'seq'}, dimensions={0}, use_global_device_ids=true | all-gather | bytes 835584 | tf_op jit(solution)/shard_map/all_gather | solution.py:113
  39.0 2.2 copy.63
  42.2 35.4 %all-gather = s32[1,2048]{1,0:T(1,128)S(1)} all-gather(s32[1,128]{1,0:T(1,128)S(1)} %copy-done.16), channel_id=2, replica_groups=mesh['ctx'=16,'seq'=16] {'ctx'}, dimensions={1}, use_global_device_ids=true | all-gather | bytes 8704 | tf_op jit(solution)/shard_map/all_gather | solution.py:152
  77.6 68.5 %all-gather.7.cloned.1.call-done = bf16[16,6,64,384]{3,2,1,0:T(8,128)(2,1)} async-done(((bf16[1,6,64,384]{3,2,1,0:T(8,128)(2,1)}), bf16[16,6,64,384]{3,2,1,0:T(8,128)(2,1)}) %all-gather.7.cloned.1.call-update) | async-done | bytes 4718608 | tf_op jit(solution)/shard_map/all_gather | solution.py:118
  146.1 2.3 slice_bitcast_fusion
  150.5 3.9 gather_fusion.1
  154.4 2.8 copy_bitcast_fusion
  159.3 2.7 fusion.34
  165.6 2.1 add_convert_fusion
  169.1 61.5 %all-gather.9.cloned.1.call-done = bf16[1,2048,512]{1,2,0:T(8,128)(2,1)} async-done(((bf16[1,128,512]{1,2,0:T(8,128)(2,1)}), bf16[1,2048,512]{1,2,0:T(8,128)(2,1)}) %all-gather.9.cloned.1.call-update) | async-done | bytes 2097168 | tf_op jit(solution)/shard_map/all_gather | solution.py:150
  230.6 85.8 %all-gather.11.cloned.1.call-done = bf16[1,2048,512]{1,2,0:T(8,128)(2,1)} async-done(((bf16[1,128,512]{1,2,0:T(8,128)(2,1)}), bf16[1,2048,512]{1,2,0:T(8,128)(2,1)}) %all-gather.11.cloned.1.call-update) | async-done | bytes 2097168 | tf_op jit(solution)/shard_map/all_gather | solution.py:151
  316.3 42.3 %while.36 = (s32[]{:T(128)}, f32[4,4,128]{2,1,0:T(4,128)S(1)}, f32[4,4,128]{2,1,0:T(4,128)S(1)}, f32[4,4,128,128]{3,2,1,0:T(8,128)}, s32[1,128]{1,0:T(1,128)S(1)...) while((s32[]{:T(128)}, f32[4,4,128]{2,1,0:T(4,128)S(1)}, ...), condition=%wide.region_3.4_spmd.clone, body=%wide.region_0.0_spmd.clone.sunk | while | flops 551496320 | bytes 43921192 | solution.py:180
  317.9 2.8 fusion.95
  320.7 3.3 fusion.96
  328.5 2.8 fusion.95
  331.3 3.3 fusion.96
  339.1 2.8 fusion.95
  341.9 3.3 fusion.96
  349.7 2.8 fusion.95
  352.5 3.3 fusion.96
  358.6 2.4 fusion.46
  362.6 2.6 broadcast.152.clone
  365.2 2.5 broadcast.152.clone2
  367.7 132.2 %while.37 = (s32[]{:T(128)}, f32[4,4,128,128]{3,2,1,0:T(8,128)}, f32[2048,512]{1,0:T(8,128)}, f32[2048,512]{1,0:T(8,128)}, s32[1,128]{1,0:T(1,128)S(1)}, /*index...) while((s32[]{:T(128)}, f32[4,4,128,128]{3,2,1,0:T(8,128)}, ...), condition=%wide.region_5.6_spmd.clone, body=%wide.region_4.5_spmd.clone.sunk | while | flops 1356530304 | bytes 85692320 | solution.py:255
  374.3 2.9 fusion.111
  377.2 2.3 constant_dynamic-slice_fusion.14
  379.5 2.5 copy.120
  382.0 3.6 fusion.112
  386.8 2.6 copy.121
  389.4 2.3 constant_dynamic-slice_fusion.15
  391.6 2.5 copy.122
  407.0 3.3 fusion.111
  410.3 2.3 constant_dynamic-slice_fusion.14
  412.5 2.5 copy.120
  415.1 3.6 fusion.112
  419.9 2.6 copy.121
  422.4 2.3 constant_dynamic-slice_fusion.15
  424.7 2.5 copy.122
  440.1 3.3 fusion.111
  443.4 2.3 constant_dynamic-slice_fusion.14
  445.7 2.5 copy.120
  448.2 3.6 fusion.112
  453.0 2.6 copy.121
  455.6 2.3 constant_dynamic-slice_fusion.15
  457.8 2.5 copy.122
  473.3 3.3 fusion.111
  476.6 2.3 constant_dynamic-slice_fusion.14
  478.9 2.5 copy.120
  481.4 3.6 fusion.112
  486.2 2.6 copy.121
  488.7 2.3 constant_dynamic-slice_fusion.15
  491.0 2.5 copy.122
  503.9 3.1 fusion.37
  509.2 4.0 scatter_fusion.1
  513.2 2.5 copy.114
  517.8 3.4 broadcast_in_dim.144
  521.2 9.0 scatter_fusion
  530.2 5.6 copy.113
  536.5 2.9 pad_maximum_fusion
  539.4 6.5 copy.74
  546.1 206.1 %reduce-scatter.9.cloned.1.call-done = f32[1,6,64,384]{3,2,1,0:T(8,128)} async-done(((f32[16,6,64,384]{3,2,1,0:T(8,128)}), f32[1,6,64,384]{3,2,1,0:T(8,128)}) %reduce-scatter.9.cloned.1.call-update) | async-done | bytes 589840 | tf_op jit(solution)/shard_map/reduce_scatter | solution.py:288
  758.2 75.2 %reduce-scatter.11.cloned.1.call-done = f32[1,64,384]{2,1,0:T(8,128)} async-done(((f32[16,64,384]{2,1,0:T(8,128)}), f32[1,64,384]{2,1,0:T(8,128)}) %reduce-scatter.11.cloned.1.call-update) | async-done | bytes 98320 | tf_op jit(solution)/shard_map/reduce_scatter | solution.py:296
  836.2 99.8 %reduce-scatter.5.cloned.1.call-done = f32[128,512]{1,0:T(8,128)} async-done(((f32[2048,512]{1,0:T(8,128)}), f32[128,512]{1,0:T(8,128)}) %reduce-scatter.5.cloned.1.call-update) | async-done | bytes 262160 | tf_op jit(solution)/shard_map/reduce_scatter | solution.py:286
  936.1 103.3 %reduce-scatter.7.cloned.1.call-done = f32[128,512]{1,0:T(8,128)} async-done(((f32[2048,512]{1,0:T(8,128)}), f32[128,512]{1,0:T(8,128)}) %reduce-scatter.7.cloned.1.call-update) | async-done | bytes 262160 | tf_op jit(solution)/shard_map/reduce_scatter | solution.py:287
  (235 shorter events, 109.6 us)
Async XLA Ops:
  7.2 152.1 %copy-start = (bf16[1,128,4096]{2,1,0:T(8,128)(2,1)S(1)}, bf16[1,128,4096]{2,1,0:T(8,128)(2,1)}, u32[]{:S(2)}) copy-start(bf16[1,128,4096]{2,1,0:T(8,128)(2,1)} %param.14) | copy-start | bytes 3145732
  7.2 34.0 %copy-start.15 = (bf16[1,128,2048]{2,1,0:T(8,128)(2,1)S(1)}, bf16[1,128,2048]{2,1,0:T(8,128)(2,1)}, u32[]{:S(2)}) copy-start(bf16[1,128,2048]{2,1,0:T(8,128)(2,1)} %param.23) | copy-start | bytes 1572868
  7.2 35.0 %copy-start.16 = (s32[1,128]{1,0:T(1,128)S(1)}, s32[1,128]{1,0:T(1,128)}, u32[]{:S(2)}) copy-start(s32[1,128]{1,0:T(1,128)} %param.18) | copy-start | bytes 1540
  7.2 70.4 %copy-start.19 = (s32[1,4]{1,0:T(1,128)S(1)}, s32[1,4]{1,0:T(1,128)}, u32[]{:S(2)}) copy-start(s32[1,4]{1,0:T(1,128)} %param.19) | copy-start | bytes 52
  7.2 138.9 %all-gather.7.cloned.1.call-start = ((), (), s32[]{:S(2)}) async-start(), calls=%async_computation.4 | async-start | bytes 5013504 | tf_op jit(solution)/shard_map/all_gather | solution.py:118
  8.2 25.7 %copy-start.17 = (s32[6]{0:T(128)}, s32[6]{0:T(128)S(1)}, u32[]{:S(2)}) copy-start(s32[6]{0:T(128)S(1)} %fusion.40) | copy-start | bytes 76
  35.4 195.2 %all-gather.9.cloned.1.call-start = ((), (), s32[]{:S(2)}) async-start(), calls=%async_computation.9 | async-start | bytes 2228224 | tf_op jit(solution)/shard_map/all_gather | solution.py:150
  37.1 279.2 %all-gather.11.cloned.1.call-start = ((), (), s32[]{:S(2)}) async-start(), calls=%async_computation.10 | async-start | bytes 2228224 | tf_op jit(solution)/shard_map/all_gather | solution.py:151
  38.9 713.3 %reduce-scatter.9.cloned.1.call-start = ((), (), s32[]{:S(2)}) async-start(), calls=%async_computation.7 | async-start | bytes 10027008 | tf_op jit(solution)/shard_map/reduce_scatter | solution.py:288
  159.2 4.8 copy-start.7
  317.9 6.2 copy-start.13
  320.7 3.4 copy-start.1
  325.9 1.0 copy-start.14
  328.5 6.2 copy-start.13
  331.3 3.4 copy-start.1
  336.5 1.0 copy-start.14
  339.1 6.2 copy-start.13
  341.9 3.4 copy-start.1
  347.0 1.0 copy-start.14
  349.6 6.2 copy-start.13
  352.5 3.4 copy-start.1
  357.6 1.0 copy-start.14
  367.7 5.0 copy-start.11
  368.8 3.6 copy-start.2
  370.8 3.5 copy-start.3
  382.0 3.6 copy-start.5
  394.2 1.9 copy-start.6
  396.1 2.8 copy-start.4
  400.4 5.0 copy-start.11
  401.5 3.6 copy-start.2
  403.5 3.4 copy-start.3
  415.1 3.6 copy-start.5
  427.2 1.9 copy-start.6
  429.2 2.8 copy-start.4
  433.5 5.0 copy-start.11
  434.6 3.6 copy-start.2
  436.6 3.5 copy-start.3
  448.2 3.6 copy-start.5
  460.4 1.9 copy-start.6
  462.3 2.8 copy-start.4
  466.7 5.0 copy-start.11
  467.8 3.6 copy-start.2
  469.8 3.4 copy-start.3
  481.4 3.6 copy-start.5
  493.6 1.9 copy-start.6
  495.5 2.8 copy-start.4
  499.9 4.1 copy-start.8
  507.0 2.2 copy-start.10
  546.0 206.3 %copy-start.18 = (s32[6]{0:T(128)S(1)}, s32[6]{0:T(128)}, u32[]{:S(2)}) copy-start(s32[6]{0:T(128)} %copy-done.17) | copy-start | bytes 76
  546.0 287.4 %reduce-scatter.11.cloned.1.call-start = ((), (), s32[]{:S(2)}) async-start(), calls=%async_computation.8 | async-start | bytes 1671168 | tf_op jit(solution)/shard_map/reduce_scatter | solution.py:296
  754.1 1.2 copy-start.9
  755.3 180.8 %reduce-scatter.5.cloned.1.call-start = ((), (), s32[]{:S(2)}) async-start(), calls=%async_computation.5 | async-start | bytes 4456448 | tf_op jit(solution)/shard_map/reduce_scatter | solution.py:286
  755.3 1.3 copy-start.12
  755.9 283.5 %reduce-scatter.7.cloned.1.call-start = ((), (), s32[]{:S(2)}) async-start(), calls=%async_computation.6 | async-start | bytes 4456448 | tf_op jit(solution)/shard_map/reduce_scatter | solution.py:287
Sparse Core Ops, SparseCore 0:
  35.5 110.5 all-gather.6
  148.4 82.0 all-gather.8
  232.9 83.4 all-gather.10
  546.1 205.9 reduce-scatter.8
  756.2 77.1 reduce-scatter.10
  836.5 99.4 reduce-scatter.4
  939.4 99.9 reduce-scatter.6
where the time goes:
time: 1050 us
  waiting for transfers between devices  701 us (67%)
  local copies, waits for them, and re-layouts  145 us (14%)
  matrix products  75.2 us (7%)
  blocking collectives  60.3 us (6%)
  other arithmetic  49.3 us (5%)
  between operations  14.4 us (1%)
    reduce_scatter x1, waiting for transfers between devices, per_device(): lax.psum_scatter(adapter_terms, 'ctx', scatter_dimension=0, tiled=True)  206 us
    reduce_scatter x1, waiting for transfers between devices, per_device(): lax.psum_scatter(value_rows_grad, 'ctx', scatter_dimension=0, tiled=True)  103 us
    reduce_scatter x1, waiting for transfers between devices, per_device(): lax.psum_scatter(key_rows_grad, 'ctx', scatter_dimension=0, tiled=True)  99.8 us
    all_gather x1, waiting for transfers between devices, per_device(): lax.all_gather(value_head_states[0], 'ctx', axis=0, tiled=True)  85.8 us
    reduce_scatter x1, waiting for transfers between devices, per_device(): lax.psum_scatter(owner_table, 'seq', scatter_dimension=0, tiled=True)  75.2 us
    all_gather x1, waiting for transfers between devices, per_device(): spread = lax.all_gather(picked[None], 'ctx', axis=0, tiled=True)  68.5 us
    all_gather x1, waiting for transfers between devices, per_device(): lax.all_gather(key_head_states[0], 'ctx', axis=0, tiled=True)  61.5 us
    all_gather x1, blocking collectives, per_device(): lax.all_gather(document_numbers[0], 'ctx', axis=0, tiled=True)  35.4 us
  transfers between devices with their start and end apart: 7, of which 7 were waited for; matrix products, arithmetic and copies ran while one was open for 3% of the time, Pallas kernels for 0%

commit v1 on v0

--- a/solution.py
+++ b/solution.py
@@ -148,7 +148,10 @@
     )
     gathered = (
         lax.all_gather(key_head_states[0], "ctx", axis=0, tiled=True),
-        lax.all_gather(value_head_states[0], "ctx", axis=0, tiled=True),
+        jnp.concatenate(
+            lax.all_to_all(jnp.stack([value_head_states[0]] * lax.axis_size("ctx")), "ctx", 0, 0),
+            axis=0,
+        ),
         lax.all_gather(document_numbers[0], "ctx", axis=0, tiled=True),
     )
     key_piece, value_piece, doc_piece = gathered

time: 1050 us -> 992 us (0.945)
  waiting for transfers between devices: 701 us -> 577 us
  blocking collectives: 60.3 us -> 112 us
    all_gather x1 -> x0, waiting for transfers between devices: 85.8 us -> none  [per_device(): lax.all_gather(value_head_states[0], 'ctx', axis=0, tiled=True)]
    all_gather x1, blocking collectives: 35.4 us -> 87.1 us  [per_device(): lax.all_gather(document_numbers[0], 'ctx', axis=0, tiled=True)]
    all_gather x1, waiting for transfers between devices: 68.5 us -> 34.1 us  [per_device(): spread = lax.all_gather(picked[None], 'ctx', axis=0, tiled=True)]
  transfers between devices with their start and end apart: 7 -> 7, of which waited for: 7 -> 6; matrix products, arithmetic and copies ran while one was open for 3% -> 4% of each run, Pallas kernels for 0% -> 0%
where the time goes in v1:
time: 992 us; the launch traced here: 990 us
  waiting for transfers between devices  577 us (58%)
  local copies, waits for them, and re-layouts  152 us (15%)
  blocking collectives  112 us (11%)
  matrix products  75.1 us (8%)
  other arithmetic  49.3 us (5%)
  between operations  14.4 us (1%)
    reduce_scatter x1, waiting for transfers between devices, per_device(): lax.psum_scatter(adapter_terms, 'ctx', scatter_dimension=0, tiled=True)  205 us
    reduce_scatter x1, waiting for transfers between devices, per_device(): lax.psum_scatter(value_rows_grad, 'ctx', scatter_dimension=0, tiled=True)  103 us
    reduce_scatter x1, waiting for transfers between devices, per_device(): lax.psum_scatter(key_rows_grad, 'ctx', scatter_dimension=0, tiled=True)  99.9 us
    all_gather x1, blocking collectives, per_device(): lax.all_gather(document_numbers[0], 'ctx', axis=0, tiled=True)  87.1 us
    reduce_scatter x1, waiting for transfers between devices, per_device(): lax.psum_scatter(owner_table, 'seq', scatter_dimension=0, tiled=True)  75.4 us
    all_gather x1, waiting for transfers between devices, per_device(): lax.all_gather(key_head_states[0], 'ctx', axis=0, tiled=True)  58.8 us
    all_gather x1, waiting for transfers between devices, per_device(): spread = lax.all_gather(picked[None], 'ctx', axis=0, tiled=True)  34.1 us
    all_gather x1, blocking collectives, per_device(): every_slice = lax.all_gather(owned_token_slices, 'seq', axis=0, tiled=True)  24.9 us
  transfers between devices with their start and end apart: 7, of which 6 were waited for; matrix products, arithmetic and copies ran while one was open for 4% of the time, Pallas kernels for 0%

profile of v1, /device:TPU:8, one launch (start us, length us, event | category | flops | bytes accessed | tf_op | source)
XLA Modules:
  0.0 989.5 jit_solution(2069719634484015387)
XLA Ops:
  9.0 24.9 %all_gather.14 = bf16[16,64,384]{2,1,0:T(8,128)(2,1)S(1)} all-gather(bf16[1,64,384]{2,1,0:T(8,128)(2,1)S(1)} %pad_maximum_fusion.1), channel_id=1, replica_groups=mesh['ctx'=16,'seq'=16] {'seq'}, dimensions={0}, use_global_device_ids=true | all-gather | bytes 835584 | tf_op jit(solution)/shard_map/all_gather | solution.py:113
  38.2 8.6 all-to-all-start
  51.9 87.1 %all-gather = s32[1,2048]{1,0:T(1,128)S(1)} all-gather(s32[1,128]{1,0:T(1,128)S(1)} %copy-done.16), channel_id=2, replica_groups=mesh['ctx'=16,'seq'=16] {'ctx'}, dimensions={1}, use_global_device_ids=true | all-gather | bytes 8704 | tf_op jit(solution)/shard_map/all_gather | solution.py:155
  139.0 2.6 copy.92
  141.7 3.9 copy.94
  145.6 34.1 %all-gather.5.cloned.1.call-done = bf16[16,6,64,384]{3,2,1,0:T(8,128)(2,1)} async-done(((bf16[1,6,64,384]{3,2,1,0:T(8,128)(2,1)}), bf16[16,6,64,384]{3,2,1,0:T(8,128)(2,1)}) %all-gather.5.cloned.1.call-update) | async-done | bytes 4718608 | tf_op jit(solution)/shard_map/all_gather | solution.py:118
  179.7 2.3 slice_bitcast_fusion
  184.1 3.9 gather_fusion.1
  187.9 2.8 copy_bitcast_fusion
  192.8 2.7 fusion.34
  202.7 58.8 %all-gather.7.cloned.1.call-done = bf16[1,2048,512]{1,2,0:T(8,128)(2,1)} async-done(((bf16[1,128,512]{1,2,0:T(8,128)(2,1)}), bf16[1,2048,512]{1,2,0:T(8,128)(2,1)}) %all-gather.7.cloned.1.call-update) | async-done | bytes 2097168 | tf_op jit(solution)/shard_map/all_gather | solution.py:150
  261.5 42.2 %while.36 = (s32[]{:T(128)}, f32[4,4,128]{2,1,0:T(4,128)S(1)}, f32[4,4,128]{2,1,0:T(4,128)S(1)}, f32[4,4,128,128]{3,2,1,0:T(8,128)}, s32[1,128]{1,0:T(1,128)S(1)...) while((s32[]{:T(128)}, f32[4,4,128]{2,1,0:T(4,128)S(1)}, ...), condition=%wide.region_3.4_spmd.clone, body=%wide.region_0.0_spmd.clone.sunk | while | flops 551496320 | bytes 43921192 | solution.py:183
  263.1 2.8 fusion.95
  265.9 3.3 fusion.96
  273.6 2.8 fusion.95
  276.5 3.3 fusion.96
  284.2 2.8 fusion.95
  287.0 3.3 fusion.96
  294.7 2.8 fusion.95
  297.6 3.3 fusion.96
  303.7 2.4 fusion.46
  307.6 2.6 broadcast.153.clone
  310.2 2.5 broadcast.153.clone2
  312.7 132.2 %while.37 = (s32[]{:T(128)}, f32[4,4,128,128]{3,2,1,0:T(8,128)}, f32[2048,512]{1,0:T(8,128)}, f32[2048,512]{1,0:T(8,128)}, s32[1,128]{1,0:T(1,128)S(1)}, /*index...) while((s32[]{:T(128)}, f32[4,4,128,128]{3,2,1,0:T(8,128)}, ...), condition=%wide.region_5.6_spmd.clone, body=%wide.region_4.5_spmd.clone.sunk | while | flops 1356530304 | bytes 85692320 | solution.py:258
  319.3 2.9 fusion.111
  322.2 2.3 constant_dynamic-slice_fusion.14
  324.5 2.5 copy.147
  327.1 3.6 fusion.112
  331.9 2.6 copy.148
  334.4 2.3 constant_dynamic-slice_fusion.15
  336.7 2.6 copy.149
  352.1 3.3 fusion.111
  355.3 2.3 constant_dynamic-slice_fusion.14
  357.6 2.5 copy.147
  360.2 3.6 fusion.112
  364.9 2.6 copy.148
  367.5 2.3 constant_dynamic-slice_fusion.15
  369.8 2.6 copy.149
  385.2 3.3 fusion.111
  388.5 2.3 constant_dynamic-slice_fusion.14
  390.7 2.5 copy.147
  393.3 3.6 fusion.112
  398.1 2.6 copy.148
  400.6 2.3 constant_dynamic-slice_fusion.15
  402.9 2.6 copy.149
  418.4 3.3 fusion.111
  421.7 2.3 constant_dynamic-slice_fusion.14
  424.0 2.5 copy.147
  426.5 3.6 fusion.112
  431.3 2.6 copy.148
  433.8 2.3 constant_dynamic-slice_fusion.15
  436.1 2.6 copy.149
  449.0 3.1 fusion.37
  454.3 3.9 scatter_fusion.1
  458.3 2.5 copy.141
  462.9 3.4 broadcast_in_dim.144
  466.3 9.0 scatter_fusion
  475.3 5.6 copy.140
  481.6 2.9 pad_maximum_fusion
  484.5 6.5 copy.101
  491.2 204.8 %reduce-scatter.9.cloned.1.call-done = f32[1,6,64,384]{3,2,1,0:T(8,128)} async-done(((f32[16,6,64,384]{3,2,1,0:T(8,128)}), f32[1,6,64,384]{3,2,1,0:T(8,128)}) %reduce-scatter.9.cloned.1.call-update) | async-done | bytes 589840 | tf_op jit(solution)/shard_map/reduce_scatter | solution.py:291
  701.9 75.4 %reduce-scatter.11.cloned.1.call-done = f32[1,64,384]{2,1,0:T(8,128)} async-done(((f32[16,64,384]{2,1,0:T(8,128)}), f32[1,64,384]{2,1,0:T(8,128)}) %reduce-scatter.11.cloned.1.call-update) | async-done | bytes 98320 | tf_op jit(solution)/shard_map/reduce_scatter | solution.py:299
  780.1 99.9 %reduce-scatter.5.cloned.1.call-done = f32[128,512]{1,0:T(8,128)} async-done(((f32[2048,512]{1,0:T(8,128)}), f32[128,512]{1,0:T(8,128)}) %reduce-scatter.5.cloned.1.call-update) | async-done | bytes 262160 | tf_op jit(solution)/shard_map/reduce_scatter | solution.py:289
  879.9 102.7 %reduce-scatter.7.cloned.1.call-done = f32[128,512]{1,0:T(8,128)} async-done(((f32[2048,512]{1,0:T(8,128)}), f32[128,512]{1,0:T(8,128)}) %reduce-scatter.7.cloned.1.call-update) | async-done | bytes 262160 | tf_op jit(solution)/shard_map/reduce_scatter | solution.py:290
  (237 shorter events, 115.0 us)
Async XLA Ops:
  7.2 185.7 %copy-start = (bf16[1,128,4096]{2,1,0:T(8,128)(2,1)S(1)}, bf16[1,128,4096]{2,1,0:T(8,128)(2,1)}, u32[]{:S(2)}) copy-start(bf16[1,128,4096]{2,1,0:T(8,128)(2,1)} %param.14) | copy-start | bytes 3145732
  7.2 172.5 %all-gather.5.cloned.1.call-start = ((), (), s32[]{:S(2)}) async-start(), calls=%async_computation.5 | async-start | bytes 5013504 | tf_op jit(solution)/shard_map/all_gather | solution.py:118
  8.2 25.7 %copy-start.17 = (s32[6]{0:T(128)}, s32[6]{0:T(128)S(1)}, u32[]{:S(2)}) copy-start(s32[6]{0:T(128)S(1)} %fusion.40) | copy-start | bytes 76
  33.9 12.9 %copy-start.15 = (bf16[1,128,512]{2,1,0:T(8,128)(2,1)S(1)}, bf16[1,128,512]{2,1,0:T(8,128)(2,1)}, u32[]{:S(2)}) copy-start(bf16[1,128,512]{2,1,0:T(8,128)(2,1)} %param.16) | copy-start | bytes 393220
  36.4 15.6 %copy-start.16 = (s32[1,128]{1,0:T(1,128)S(1)}, s32[1,128]{1,0:T(1,128)}, u32[]{:S(2)}) copy-start(s32[1,128]{1,0:T(1,128)} %param.18) | copy-start | bytes 1540
  36.4 102.6 %copy-start.19 = (s32[1,4]{1,0:T(1,128)S(1)}, s32[1,4]{1,0:T(1,128)}, u32[]{:S(2)}) copy-start(s32[1,4]{1,0:T(1,128)} %param.19) | copy-start | bytes 52
  38.2 100.9 %all-to-all-start = ((bf16[16,128,512]{1,2,0:T(8,128)(2,1)}), bf16[16,128,512]{1,2,0:T(8,128)(2,1)S(1)}, u32[]{:S(2)}, u32[]{:S(2)}) async-start(bf16[16,128,512]{1,2,0:T(8,128)(2,1)} %stack.3), calls=%async_computation | async-start | bytes 4194304 | tf_op jit(solution)/shard_map/all_to_all | solution.py:152
  46.7 214.8 %all-gather.7.cloned.1.call-start = ((), (), s32[]{:S(2)}) async-start(), calls=%async_computation.10 | async-start | bytes 2228224 | tf_op jit(solution)/shard_map/all_gather | solution.py:150
  47.6 648.4 %reduce-scatter.9.cloned.1.call-start = ((), (), s32[]{:S(2)}) async-start(), calls=%async_computation.8 | async-start | bytes 10027008 | tf_op jit(solution)/shard_map/reduce_scatter | solution.py:291
  192.8 4.8 copy-start.7
  263.1 6.2 copy-start.13
  265.9 3.4 copy-start.1
  271.0 1.0 copy-start.14
  273.6 6.2 copy-start.13
  276.4 3.4 copy-start.1
  281.6 1.0 copy-start.14
  284.2 6.2 copy-start.13
  287.0 3.4 copy-start.1
  292.1 1.0 copy-start.14
  294.7 6.2 copy-start.13
  297.6 3.4 copy-start.1
  302.7 1.0 copy-start.14
  312.7 5.0 copy-start.11
  313.9 3.6 copy-start.2
  315.9 3.4 copy-start.3
  327.1 3.6 copy-start.5
  339.2 1.9 copy-start.6
  341.2 2.8 copy-start.4
  345.5 5.0 copy-start.11
  346.6 3.6 copy-start.2
  348.6 3.4 copy-start.3
  360.2 3.6 copy-start.5
  372.3 2.0 copy-start.6
  374.3 2.8 copy-start.4
  378.6 5.0 copy-start.11
  379.7 3.6 copy-start.2
  381.7 3.5 copy-start.3
  393.3 3.6 copy-start.5
  405.4 1.9 copy-start.6
  407.4 2.8 copy-start.4
  411.8 5.0 copy-start.11
  412.9 3.6 copy-start.2
  414.9 3.4 copy-start.3
  426.5 3.6 copy-start.5
  438.7 2.0 copy-start.6
  440.6 2.8 copy-start.4
  445.0 4.1 copy-start.8
  452.2 2.2 copy-start.10
  491.1 205.0 %copy-start.18 = (s32[6]{0:T(128)S(1)}, s32[6]{0:T(128)}, u32[]{:S(2)}) copy-start(s32[6]{0:T(128)} %copy-done.17) | copy-start | bytes 76
  491.1 286.1 %reduce-scatter.11.cloned.1.call-start = ((), (), s32[]{:S(2)}) async-start(), calls=%async_computation.9 | async-start | bytes 1671168 | tf_op jit(solution)/shard_map/reduce_scatter | solution.py:299
  697.9 1.2 copy-start.9
  699.1 180.8 %reduce-scatter.5.cloned.1.call-start = ((), (), s32[]{:S(2)}) async-start(), calls=%async_computation.6 | async-start | bytes 4456448 | tf_op jit(solution)/shard_map/reduce_scatter | solution.py:289
  699.2 1.1 copy-start.12
  699.7 283.0 %reduce-scatter.7.cloned.1.call-start = ((), (), s32[]{:S(2)}) async-start(), calls=%async_computation.7 | async-start | bytes 4456448 | tf_op jit(solution)/shard_map/reduce_scatter | solution.py:290
Sparse Core Ops, SparseCore 0:
  35.5 144.2 all-gather.4
  182.0 79.4 all-gather.6
  491.2 204.6 reduce-scatter.8
  700.0 77.1 reduce-scatter.10
  780.4 99.5 reduce-scatter.4
  883.1 99.5 reduce-scatter.6
